TPU v7x, 32 devices: a whole 2x2x4 slice. The times are simulated.
32 devices in a mesh: row: 16 (over z, y, x), col: 2 (over core).
Axes of the slice: x: 2, y: 2, z: 4, core: 2. Of those that a mesh axis runs over, the one named last changes fastest.
Arguments:
- panel_u: bfloat16 [16, 2560, 128], P('row'), may hold values from -0.125 to 0.125
- panel_v: bfloat16 [16, 2560, 128], P('row', 'col'), may hold values from -0.25 to 0.25
- linv: bfloat16 [2560, 2560], P('row', 'col')
- trail_u: bfloat16 [16, 4, 2560, 128], P('row', 'col'), may hold values from -0.125 to 0.125
- trail_v: bfloat16 [16, 4, 2560, 128], P('row', 'col'), may hold values from -0.125 to 0.125
- rank_map: int32 [16, 16], replicated, may hold values from 32 to 128, as said below
- tile_of_slot: int32 [16], replicated, may hold values from 0 to 15, each once
- band_cols: int32 [4], P('col'), may hold values from 0 to 15, as said below
Outputs:
- gram_left: float32 [16, 4, 256, 256], P('row', 'col')
- gram_right: float32 [16, 4, 256, 256], P('row', 'col')
Inputs may be any that keep to these rules, and one draw needn't show every extreme that they name: rank_map[i, j] for j != i is the rank of trailing tile (i, j), including band tiles with j > i, whose core is zero; rank_map[i, i] is the rank of panel tile i; some panel tile has rank 128. `tile_of_slot`: a permutation. `band_cols`: distinct values.
All inputs are finite; a program needn't handle non-finite values.
Results may differ from a plain program's by a relative error of at most 0.0049.
Values may be sent and summed in bfloat16 or wider, within the bound.
No kernel may reach another device: no remote copies, remote signals or barrier semaphores. Data moves between devices by JAX's collectives and lax.ppermute only.
A program may use at most 64 MiB of HBM per device.

v0:
```python
import jax
import jax.numpy as jnp
from jax import lax
from jax.sharding import PartitionSpec as P


def broadcast(block, axis, holder):
    block = jnp.where(lax.axis_index(axis) == holder, block, jnp.zeros_like(block))
    return lax.psum(block, axis)


def cross_rows(first, second):
    return lax.dot_general(
        first, second, (((0,), (0,)), ((), ())), preferred_element_type=jnp.float32
    )


def shards(panel_u, panel_v, linv, trail_u, trail_v, rank_map, tile_of_slot, band_cols):
    tile_count = tile_of_slot.shape[0]
    rank_width = panel_u.shape[2]
    band_width = band_cols.shape[0]
    slot_ids = jnp.arange(tile_count, dtype=jnp.int32)
    row_ids = slot_ids[:, None]
    col_ids = slot_ids[None, :]
    columns = jnp.arange(rank_width, dtype=jnp.int32)

    def rank_lookup(first_tile, second_tile):
        return jnp.sum(jnp.where((row_ids == first_tile) & (col_ids == second_tile), rank_map, 0))

    own_slot = lax.axis_index("row")
    own_tile = jnp.sum(jnp.where(slot_ids == own_slot, tile_of_slot, 0))
    own_keep = (columns < rank_lookup(own_tile, own_tile))[None, :]
    own_basis = jnp.where(own_keep, panel_u[0], jnp.zeros_like(panel_u[0]))
    own_right = jnp.where(own_keep, panel_v[0], jnp.zeros_like(panel_v[0]))
    band_tiles = [band_cols[band_slot] for band_slot in range(band_width)]
    sources = [
        jnp.sum(jnp.where(tile_of_slot == band_tile, slot_ids, 0)) for band_tile in band_tiles
    ]
    partial_value = jnp.dot(
        lax.all_gather(linv, "row", axis=0, tiled=True),
        own_right,
        preferred_element_type=jnp.float32,
    )
    solved = lax.psum(partial_value, "col").astype(jnp.bfloat16)
    pairs = [
        (
            broadcast(own_basis, "row", sources[band_slot]),
            broadcast(solved, "row", sources[band_slot]),
        )
        for band_slot in range(band_width)
    ]
    bases = [pair_now[0] for pair_now in pairs]
    weights = [pair_now[1] for pair_now in pairs]
    left_grams = []
    right_grams = []
    for band_slot in range(band_width):
        band_tile = band_tiles[band_slot]
        core_mat = cross_rows(solved, weights[band_slot])
        core_mat = jnp.where(band_tile < own_tile, core_mat, jnp.zeros_like(core_mat)).astype(
            jnp.bfloat16
        )
        update = jnp.dot(bases[band_slot], core_mat.T, preferred_element_type=jnp.float32).astype(
            jnp.bfloat16
        )
        trail_keep = (columns < rank_lookup(own_tile, band_tile))[None, :]
        kept_u = jnp.where(trail_keep, trail_u[0, band_slot], jnp.zeros_like(update))
        kept_v = jnp.where(trail_keep, trail_v[0, band_slot], jnp.zeros_like(update))
        left_stack = jnp.concatenate([kept_u, own_basis], axis=1)
        right_stack = jnp.concatenate([kept_v, -update], axis=1)
        left_grams.append(cross_rows(left_stack, left_stack))
        right_grams.append(cross_rows(right_stack, right_stack))
    return (jnp.stack(left_grams, axis=0)[None], jnp.stack(right_grams, axis=0)[None])


def solution(mesh):
    return jax.shard_map(
        shards,
        mesh=mesh,
        in_specs=(
            P("row", None, None),
            P("row", "col", None),
            P("row", "col"),
            P("row", "col", None, None),
            P("row", "col", None, None),
            P(),
            P(),
            P("col"),
        ),
        out_specs=(P("row", "col", None, None), P("row", "col", None, None)),
        check_vma=False,
    )
```

profile of v0, /device:TPU:0, one launch (start us, length us, event | category | flops | bytes accessed | tf_op | source)
XLA Modules:
  0.0 272.0 jit_solution(12180962195053194650)
XLA Ops:
  7.2 0.7 all-gather.2.cloned.1.call-update
  8.0 1.3 fusion.42
  9.3 2.6 fusion.31
  15.7 1.3 copy.11
  17.1 1.1 copy.15
  18.5 0.7 iota_compare_fusion
  20.4 0.8 select_reduce_fusion.2
  21.8 1.0 broadcast_select_fusion.3
  22.8 0.9 broadcast_select_fusion.1
  23.7 85.6 %all-gather.2.cloned.1.call-done = bf16[2560,1280]{1,0:T(8,128)(2,1)} async-done(((bf16[160,1280]{1,0:T(8,128)(2,1)}), bf16[2560,1280]{1,0:T(8,128)(2,1)}) %all-gather.2.cloned.1.call-update) | async-done | bytes 6553616 | tf_op jit(solution)/shard_map/all_gather | solution.py:40
  109.3 5.1 %convolution_bitcast_fusion = f32[2560,128]{0,1:T(8,128)S(1)} fusion(bf16[2560,1280]{1,0:T(8,128)(2,1)} %all-gather.2.cloned.1.call-done, bf16[1,1280,128]{2,1,0:T(8,128)(2,1)S(1)} %copy-done.5, pred[128]{0:T(512)(128)(4,1)S(1)} %iota_compare_fusion.2), kind=kOutput, calls=%fused_computation | convolution fusion | flops 839024640 | bytes 8192128 | tf_op jit(solution)/shard_map/dot_general | solution.py:39
  114.4 7.0 %all-reduce.5 = bf16[2560,128]{0,1:T(8,128)(2,1)S(1)} all-reduce(f32[2560,128]{0,1:T(8,128)S(1)} %convolution_bitcast_fusion), channel_id=1, replica_groups=mesh['row'=16,'col'=2] {'col'}, use_global_device_ids=true, to_apply=%region_6.7 | all-reduce | flops 327680 | bytes 1966080 | tf_op jit(solution)/shard_map/psum | solution.py:44
  121.4 1.2 broadcast_select_fusion.2
  122.6 1.4 fusion.40
  124.0 1.1 copy.17
  125.1 1.1 copy.18
  126.2 1.3 iota_compare_fusion.1
  127.5 1.2 bitcast_select_fusion.1
  130.5 0.8 maximum_bitcast_fusion
  131.4 126.5 %all-reduce.4.cloned.1.call-done = (bf16[2560,128]{0,1:T(8,128)(2,1)}, bf16[2560,128]{0,1:T(8,128)(2,1)}, bf16[2560,128]{0,1:T(8,128)(2,1)}, bf16[2560,128]{0,1:T(8,128)(2,1)}) async-done(((bf16[2560,128]{0,1:T(8,128)(2,1)}, bf16[2560,128]{0,1:T(8,128)(2,1)}, bf16[2560,128]{0,1:T(8,128)(2,1)}, bf16[2560,128]{0,1:T(8,128)(2,1)}), (bf16[2560,128]{0,1:T(8,128)(2,1)}, bf16[2560,128]{0,1:T(8,128)(2,1)}, ...) | async-done | bytes 2621456 | tf_op jit(solution)/shard_map/psum | solution.py:9
  257.9 3.0 %fusion = bf16[2560,128]{0,1:T(8,128)(2,1)} fusion(bf16[2560,128]{0,1:T(8,128)(2,1)} %get-tuple-element.10, bf16[2560,128]{0,1:T(8,128)(2,1)S(1)} %all-reduce.5, bf16[2560,128]{0,1:T(8,128)(2,1)} %get-tuple-element.11, pred[]{:T(512)S(6)} %lt.42), kind=kOutput, calls=%fused_computation.3 | convolution fusion | flops 169115648 | bytes 2621441 | tf_op jit(solution)/shard_map/dot_general | solution.py:62
  260.9 1.9 fusion.17
  262.9 0.9 fusion.1
  264.3 0.8 maximum_bitcast_fusion.1
  (26 shorter events, 4.6 us)
Async XLA Ops:
  7.2 9.8 %copy-start.2 = (bf16[1,2,2560,128]{3,2,1,0:T(8,128)(2,1)S(1)}, bf16[1,2,2560,128]{3,2,1,0:T(8,128)(2,1)}, u32[]{:S(2)}) copy-start(bf16[1,2,2560,128]{3,2,1,0:T(8,128)(2,1)} %param.11) | copy-start | bytes 3932164
  7.2 102.1 %all-gather.2.cloned.1.call-start = ((), (), s32[]{:S(2)}) async-start(), calls=%async_computation | async-start | bytes 6963200 | tf_op jit(solution)/shard_map/all_gather | solution.py:40
  7.9 250.0 %all-reduce.4.cloned.1.call-start = ((), (), s32[]{:S(2)}) async-start(), calls=%async_computation.1 | async-start | bytes 5242880 | tf_op jit(solution)/shard_map/psum | solution.py:9
  17.1 3.3 %copy-start.6 = (s32[16,16]{1,0:T(8,128)S(1)}, s32[16,16]{1,0:T(8,128)}, u32[]{:S(2)}) copy-start(s32[16,16]{1,0:T(8,128)} %param.13) | copy-start | bytes 3076
  21.8 87.5 %copy-start.5 = (bf16[1,1280,128]{2,1,0:T(8,128)(2,1)S(1)}, bf16[1,1280,128]{2,1,0:T(8,128)(2,1)}, u32[]{:S(2)}) copy-start(bf16[1,1280,128]{2,1,0:T(8,128)(2,1)} %param.9) | copy-start | bytes 983044
  125.1 2.4 copy-start
  128.7 1.1 copy-start.1
  260.9 1.9 copy-start.3
  260.9 1.9 copy-start.4
Sparse Core Ops, SparseCore 0:
  10.7 98.6 all-gather.1
  122.7 135.1 all-reduce.3
where the time goes:
time: 273 us; the launch traced here: 272 us
  waiting for transfers between devices  213 us (78%)
  between operations  18 us (7%)
  other arithmetic  13.4 us (5%)
  matrix products  12.6 us (5%)
  local copies, waits for them, and re-layouts  8.19 us (3%)
  blocking collectives  6.96 us (3%)
    psum x1, waiting for transfers between devices, broadcast(): return lax.psum(block, axis)  127 us
    all_gather x1, waiting for transfers between devices, shards(): lax.all_gather(linv, 'row', axis=0, tiled=True)  85.6 us
    psum x1, blocking collectives, shards(): solved = lax.psum(partial_value, 'col').astype(jnp.bfloat16)  6.96 us
  transfers between devices with their start and end apart: 2, of which 2 were waited for; matrix products, arithmetic and copies ran while one was open for 7% of the time, Pallas kernels for 0%

commit v1 on v0

--- a/solution.py
+++ b/solution.py
@@ -6,7 +6,7 @@
 
 def broadcast(block, axis, holder):
     block = jnp.where(lax.axis_index(axis) == holder, block, jnp.zeros_like(block))
-    return lax.psum(block, axis)
+    return jnp.sum(lax.all_gather(block, axis), axis=0)
 
 
 def cross_rows(first, second):

time: 273 us -> 674 us (2.47)
  waiting for transfers between devices: 213 us -> 559 us
  other arithmetic: 13.4 us -> 45.2 us
  local copies, waits for them, and re-layouts: 8.19 us -> 32.8 us
    all_gather x0 -> x4, waiting for transfers between devices: none -> 468 us  [broadcast(): return jnp.sum(lax.all_gather(block, axis), axis=0)]
    psum x1 -> x0, waiting for transfers between devices: 127 us -> none  [broadcast(): return lax.psum(block, axis)]
    reduce_sum x0 -> x4, other arithmetic: none -> 29.8 us  [broadcast(): return jnp.sum(lax.all_gather(block, axis), axis=0)]
    unnamed x19, local copies, waits for them, and re-layouts: 5.42 us -> 28.7 us
  transfers between devices with their start and end apart: 2 -> 5, of which waited for: 2 -> 5; matrix products, arithmetic and copies ran while one was open for 7% -> 9% of each run, Pallas kernels for 0% -> 0%
where the time goes in v1:
time: 674 us
  waiting for transfers between devices  559 us (83%)
  other arithmetic  45.2 us (7%)
  local copies, waits for them, and re-layouts  32.8 us (5%)
  between operations  17.8 us (3%)
  matrix products  11.7 us (2%)
  blocking collectives  6.96 us (1%)
    all_gather x4, waiting for transfers between devices, broadcast(): return jnp.sum(lax.all_gather(block, axis), axis=0)  468 us
    all_gather x1, waiting for transfers between devices, shards(): lax.all_gather(linv, 'row', axis=0, tiled=True)  88.9 us
    reduce_sum x4, other arithmetic, broadcast(): return jnp.sum(lax.all_gather(block, axis), axis=0)  29.8 us
    unnamed x19, local copies, waits for them, and re-layouts  28.7 us
  transfers between devices with their start and end apart: 5, of which 5 were waited for; matrix products, arithmetic and copies ran while one was open for 9% of the time, Pallas kernels for 0%

profile of v1, /device:TPU:0, one launch (start us, length us, event | category | flops | bytes accessed | tf_op | source)
XLA Modules:
  0.0 673.6 jit_solution(1014953119871382980)
XLA Ops:
  7.9 1.3 fusion.42
  9.3 2.7 fusion.31
  15.2 1.5 select_reduce_fusion.2
  17.3 2.3 broadcast_select_fusion.4
  20.4 88.9 %all-gather.10.cloned.1.call-done = bf16[2560,1280]{1,0:T(8,128)(2,1)} async-done(((bf16[160,1280]{1,0:T(8,128)(2,1)}), bf16[2560,1280]{1,0:T(8,128)(2,1)}) %all-gather.10.cloned.1.call-update) | async-done | bytes 6553616 | tf_op jit(solution)/shard_map/all_gather | solution.py:40
  109.3 5.1 convolution_bitcast_fusion
  114.5 7.0 %all-reduce.1 = bf16[2560,128]{0,1:T(8,128)(2,1)S(1)} all-reduce(f32[2560,128]{0,1:T(8,128)S(1)} %convolution_bitcast_fusion), channel_id=1, replica_groups=mesh['row'=16,'col'=2] {'col'}, use_global_device_ids=true, to_apply=%region_6.7 | all-reduce | flops 327680 | bytes 1966080 | tf_op jit(solution)/shard_map/psum | solution.py:44
  121.4 1.2 broadcast_select_fusion.2
  126.1 1.4 fusion.41
  127.4 1.1 copy.20
  128.8 1.4 fusion.40
  132.4 1.3 iota_compare_fusion.1
  138.3 103.7 %all-gather.8.cloned.1.call-done = bf16[16,2560,128]{2,1,0:T(8,128)(2,1)} async-done(((bf16[1,2560,128]{2,1,0:T(8,128)(2,1)}), bf16[16,2560,128]{2,1,0:T(8,128)(2,1)}) %all-gather.8.cloned.1.call-update) | async-done | bytes 10485776 | tf_op jit(solution)/shard_map/all_gather | solution.py:9
  242.0 5.8 reduce_sum.107
  247.8 126.6 %all-gather.12.cloned.1.call-done = bf16[16,2560,128]{2,1,0:T(8,128)(2,1)} async-done(((bf16[1,2560,128]{2,1,0:T(8,128)(2,1)}), bf16[16,2560,128]{2,1,0:T(8,128)(2,1)}) %all-gather.12.cloned.1.call-update) | async-done | bytes 10485776 | tf_op jit(solution)/shard_map/all_gather | solution.py:9
  374.4 5.8 reduce_sum.110
  380.2 126.3 %all-gather.14.cloned.1.call-done = bf16[40960,128]{0,1:T(8,128)(2,1)} async-done(((bf16[2560,128]{0,1:T(8,128)(2,1)}), bf16[40960,128]{0,1:T(8,128)(2,1)}) %all-gather.14.cloned.1.call-update) | async-done | bytes 10485776 | tf_op jit(solution)/shard_map/all_gather | solution.py:9
  506.5 12.2 %copy.24 = bf16[16,8,16,2560]{3,2,1,0:T(8,128)(2,1)} copy(bf16[16,8,16,2560]{3,1,2,0:T(8,128)(2,1)} %bitcast.46) | data formatting | bytes 20971520
  518.7 9.1 %bitcast_reduce_fusion.1 = bf16[2560,128]{0,1:T(8,128)(2,1)S(1)} fusion(bf16[16,8,16,2560]{3,2,1,0:T(8,128)(2,1)} %copy.24), kind=kLoop, calls=%fused_computation.1 | loop fusion | flops 4915200 | bytes 11141120 | tf_op jit(solution)/shard_map/reduce_sum | solution.py:9
  527.8 111.7 %all-gather.16.cloned.1.call-done = bf16[40960,128]{0,1:T(8,128)(2,1)} async-done(((bf16[2560,128]{0,1:T(8,128)(2,1)}), bf16[40960,128]{0,1:T(8,128)(2,1)}) %all-gather.16.cloned.1.call-update) | async-done | bytes 10485776 | tf_op jit(solution)/shard_map/all_gather | solution.py:9
  639.5 11.9 %copy.25 = bf16[16,8,16,2560]{3,2,1,0:T(8,128)(2,1)} copy(bf16[16,8,16,2560]{3,1,2,0:T(8,128)(2,1)} %bitcast.47) | data formatting | bytes 20971520
  651.4 9.1 %bitcast_reduce_fusion = bf16[2560,128]{0,1:T(8,128)(2,1)S(1)} fusion(bf16[16,8,16,2560]{3,2,1,0:T(8,128)(2,1)} %copy.25), kind=kLoop, calls=%fused_computation | loop fusion | flops 4915200 | bytes 11141120 | tf_op jit(solution)/shard_map/reduce_sum | solution.py:9
  660.6 1.8 fusion
  662.3 2.3 fusion.17
  (39 shorter events, 14.4 us)
Async XLA Ops:
  7.2 102.2 %all-gather.10.cloned.1.call-start = ((), (), s32[]{:S(2)}) async-start(), calls=%async_computation.1 | async-start | bytes 6963200 | tf_op jit(solution)/shard_map/all_gather | solution.py:40
  7.9 234.1 %all-gather.8.cloned.1.call-start = ((), (), s32[]{:S(2)}) async-start(), calls=%async_computation | async-start | bytes 11141120 | tf_op jit(solution)/shard_map/all_gather | solution.py:9
  17.3 92.0 %copy-start.5 = (bf16[1,1280,128]{2,1,0:T(8,128)(2,1)S(1)}, bf16[1,1280,128]{2,1,0:T(8,128)(2,1)}, u32[]{:S(2)}) copy-start(bf16[1,1280,128]{2,1,0:T(8,128)(2,1)} %param.9) | copy-start | bytes 983044
  19.6 354.8 %all-gather.12.cloned.1.call-start = ((), (), s32[]{:S(2)}) async-start(), calls=%async_computation.2 | async-start | bytes 11141120 | tf_op jit(solution)/shard_map/all_gather | solution.py:9
  20.4 486.1 %all-gather.14.cloned.1.call-start = ((), (), s32[]{:S(2)}) async-start(), calls=%async_computation.3 | async-start | bytes 11141120 | tf_op jit(solution)/shard_map/all_gather | solution.py:9
  121.4 4.4 copy-start
  122.7 516.8 %all-gather.16.cloned.1.call-start = ((), (), s32[]{:S(2)}) async-start(), calls=%async_computation.4 | async-start | bytes 11141120 | tf_op jit(solution)/shard_map/all_gather | solution.py:9
  131.3 2.6 copy-start.1
  132.4 1.5 copy-start.3
  134.9 1.1 copy-start.2
  664.6 1.1 copy-start.4
Sparse Core Ops, SparseCore 0:
  10.7 98.6 all-gather.9
  112.0 129.9 all-gather.7
  244.7 129.6 all-gather.11
  377.0 129.4 all-gather.13
  509.1 130.4 all-gather.15
